TPU v7x, 32 devices: a whole 2x2x4 slice. The times are simulated.
32 devices in a mesh: pb: 8 (over y, x, core), ga: 4 (over z).
Axes of the slice: x: 2, y: 2, z: 4, core: 2. Of those that a mesh axis runs over, the one named last changes fastest.
Arguments:
- query_points: float32 [3, 32768], P(None, 'pb'), may hold values from 0 to 1
- cotangent: bfloat16 [64, 32768], P(None, 'pb'), may hold values from -6 to 6
- slab_ids: int32 [8, 32768], P(None, 'pb'), may hold values from -1 to 3
- rel_cells: int32 [8, 32768], P(None, 'pb'), may hold values from 0 to 511
- offsets: int32 [4, 256], P('ga', 'pb'), may hold values from 0 to 15872
- latent: bfloat16 [4, 64, 16384], P('ga', None, 'pb'), may hold values from -6 to 6
- w_in: float32 [80, 6], replicated, may hold values from -2.5 to 2.5
- b_in: float32 [80], replicated, may hold values from -3 to 3
- w_out: bfloat16 [64, 80], replicated, may hold values from -0.625 to 0.625
- b_out: float32 [64], replicated, may hold values from -3 to 3
Outputs:
- grid_grad: float32 [4, 64, 16384], P('ga', None, 'pb')
- w_in_grad: float32 [80, 6], replicated
- b_in_grad: float32 [80], replicated
- w_out_grad: float32 [64, 80], replicated
- b_out_grad: float32 [64], replicated
Inputs may be any that keep to these rules, and one draw needn't show every extreme that they name: `slab_ids`: -1 marks a padding slot; otherwise the slab that holds the neighbour cell.
All inputs are finite; a program needn't handle non-finite values.
Results may differ from a plain program's by a relative error of at most 0.0085.
Values may be sent and summed in bfloat16 or wider, within the bound.
No kernel may reach another device: no remote copies, remote signals or barrier semaphores. Data moves between devices by JAX's collectives and lax.ppermute only.
A program may use at most 64 MiB of HBM per device.

v0:
```python
import math

import jax
import jax.numpy as jnp
from jax import lax
from jax.sharding import PartitionSpec as P

KN = 8
TILE = 128
WIN = 512
GX = 64
ZS = 4


def gelu_exact(values):
    return jax.nn.gelu(values, approximate=False)


def shards(query_points, cotangent, slab_ids, rel_cells, offsets, latent, w_in, b_in, w_out, b_out):
    channels = latent.shape[1]
    slab_feats = lax.all_gather(latent, "pb", axis=2, tiled=True)[0]
    cells_slab = slab_feats.shape[1]
    slab_here = lax.axis_index("ga")
    queries_dev = query_points.shape[1]
    tiles_dev = queries_dev // TILE
    per_block = math.gcd(tiles_dev, 4)
    blocks = tiles_dev // per_block
    entries = KN * TILE

    def reshape_tiles(values):
        leading = values.shape[0]
        return values.reshape(leading, blocks, per_block, TILE).transpose(1, 2, 0, 3)

    def tile_work(anchor, points, cot_cols, slabs, rels):
        window = lax.dynamic_slice_in_dim(slab_feats, anchor, WIN, 1)
        rel_flat = rels.reshape(-1)
        live_flat = slabs.reshape(-1) == slab_here
        onehot = (
            (lax.broadcasted_iota(jnp.int32, (WIN, entries), 0) == rel_flat[None, :])
            & live_flat[None, :]
        ).astype(jnp.bfloat16)
        feats = jnp.dot(window, onehot, preferred_element_type=jnp.float32)
        cell = anchor + rel_flat
        along_x = cell // (GX * ZS)
        along_y = cell // ZS % GX
        along_z = cell % ZS + slab_here * ZS
        centres = jnp.stack(
            [
                (along_x.astype(jnp.float32) + 0.5) / GX,
                (along_y.astype(jnp.float32) + 0.5) / GX,
                (along_z.astype(jnp.float32) + 0.5) / GX,
            ],
            0,
        )
        features_in = jnp.concatenate([jnp.tile(points, (1, KN)), centres], 0)
        mask_flat = live_flat.astype(jnp.float32)
        cot_flat = jnp.tile(cot_cols.astype(jnp.float32), (1, KN))
        preact = (
            jnp.dot(
                w_in,
                features_in,
                precision=lax.Precision.HIGHEST,
                preferred_element_type=jnp.float32,
            )
            + b_in[:, None]
        )
        hidden = gelu_exact(preact).astype(jnp.bfloat16)
        kernel = jnp.dot(w_out, hidden, preferred_element_type=jnp.float32) + b_out[:, None]
        grad_cell = (kernel * cot_flat * mask_flat).astype(jnp.bfloat16)
        grad_kernel = (feats * cot_flat * mask_flat).astype(jnp.bfloat16)
        window_grad = lax.dot_general(
            grad_cell, onehot, (((1,), (1,)), ((), ())), preferred_element_type=jnp.float32
        )
        grad_w_out = lax.dot_general(
            grad_kernel, hidden, (((1,), (1,)), ((), ())), preferred_element_type=jnp.float32
        )
        grad_b_out = jnp.sum(grad_kernel.astype(jnp.float32), 1)
        grad_hidden = lax.dot_general(
            w_out, grad_kernel, (((0,), (0,)), ((), ())), preferred_element_type=jnp.float32
        )
        grad_pre = jax.vjp(gelu_exact, preact)[1](grad_hidden)[0]
        grad_w_in = lax.dot_general(
            grad_pre,
            features_in,
            (((1,), (1,)), ((), ())),
            precision=lax.Precision.HIGHEST,
            preferred_element_type=jnp.float32,
        )
        grad_b_in = jnp.sum(grad_pre, 1)
        return (window_grad, grad_w_in, grad_b_in, grad_w_out, grad_b_out)

    def advance(running, inputs_block):
        partial_grad, totals = running
        anchors, points, cot_cols, slabs, rels = inputs_block
        results = jax.vmap(tile_work)(anchors, points, cot_cols, slabs, rels)
        for number in range(per_block):
            current = lax.dynamic_slice_in_dim(partial_grad, anchors[number], WIN, 1)
            partial_grad = lax.dynamic_update_slice_in_dim(
                partial_grad, current + results[0][number], anchors[number], 1
            )
        totals = tuple((old + jnp.sum(new, 0) for old, new in zip(totals, results[1:])))
        return ((partial_grad, totals), None)

    start_totals = (
        jnp.zeros((w_in.shape[0], 6), jnp.float32),
        jnp.zeros((w_in.shape[0],), jnp.float32),
        jnp.zeros((channels, w_in.shape[0]), jnp.float32),
        jnp.zeros((channels,), jnp.float32),
    )
    start_grid = jnp.zeros((channels, cells_slab), jnp.float32)
    inputs_all = (
        offsets[0].reshape(blocks, per_block),
        reshape_tiles(query_points),
        reshape_tiles(cotangent),
        reshape_tiles(slab_ids),
        reshape_tiles(rel_cells),
    )
    (partial_grad, totals), _ = lax.scan(advance, (start_grid, start_totals), inputs_all)
    owned = lax.psum_scatter(partial_grad, "pb", scatter_dimension=1, tiled=True)
    sums = lax.psum((totals[0], totals[1], totals[2], totals[3]), ("pb", "ga"))
    scale = float(queries_dev * lax.axis_size("pb")) ** (-0.5)
    return (owned[None], sums[0] * scale, sums[1] * scale, sums[2] * scale, sums[3] * scale)


def solution(mesh):
    return jax.shard_map(
        shards,
        mesh=mesh,
        in_specs=(
            P(None, "pb"),
            P(None, "pb"),
            P(None, "pb"),
            P(None, "pb"),
            P("ga", "pb"),
            P("ga", None, "pb"),
            P(),
            P(),
            P(),
            P(),
        ),
        out_specs=(P("ga", None, "pb"), P(), P(), P(), P()),
        check_vma=False,
    )
```

profile of v0, /device:TPU:0, one launch (start us, length us, event | category | flops | bytes accessed | tf_op | source)
XLA Modules:
  0.0 460.4 jit_solution(14225851162701294720)
XLA Ops:
  12.2 28.2 %all-gather.2.cloned.1.call-done = bf16[1,64,16384]{2,1,0:T(8,128)(2,1)} async-done(((bf16[1,64,2048]{2,1,0:T(8,128)(2,1)}), bf16[1,64,16384]{2,1,0:T(8,128)(2,1)}) %all-gather.2.cloned.1.call-update) | async-done | bytes 2097168 | tf_op jit(solution)/shard_map/all_gather | solution.py:21
  40.4 2.3 broadcast_in_dim.12
  42.7 359.0 %while.26 = (s32[]{:T(128)}, f32[64,16384]{1,0:T(8,128)}, f32[80,6]{0,1:T(8,128)S(1)}, f32[80]{0:T(128)S(1)}, f32[64,80]{1,0:T(8,128)S(1)}, /*index=5*/f32[64]{0...) while((s32[]{:T(128)}, f32[64,16384]{1,0:T(8,128)}, ...), condition=%wide.region_3.4_spmd.clone, body=%wide.region_0.3_spmd.clone.sunk | while | flops 747289728 | bytes 25849020 | solution.py:118
  52.8 8.9 %while.27 = (s32[]{:T(128)}, bf16[64,16384]{1,0:T(8,128)(2,1)}, s32[4,2]{0,1:T(2,128)S(1)}, bf16[4,64,512]{2,1,0:T(8,128)(2,1)S(1)}, s32[]{:T(128)}) while((s32[]{:T(128)}, bf16[64,16384]{1,0:T(8,128)(2,1)}, s32[4,2]{0,1:T(2,128)S(1)}, bf16[4,64,512]{2,1,0:T(8,128)(2,1)S(1)}, s32[]{:T(128)}) %tuple.81), condition=%wide.while_cond, body=%wide.while_body.sunk | while | flops 2 | bytes 131177 | solution.py:35
  62.0 2.2 convert_reduce_fusion.2
  64.3 5.4 %fusion.121 = (bf16[4,80,1024]{2,1,0:T(8,128)(2,1)S(1)}, f32[4,80,1024]{2,1,0:T(8,128)}, f32[4,1024,80]{1,2,0:T(8,128)}) fusion(f32[80]{0:T(128)S(1)} %get-tuple-element.726, f32[80,6]{0,1:T(8,128)S(1)} %get-tuple-element.725, f32[4,6,1024]{2,0,1:T(4,128)S(1)} %pad_maximum_fusion.2), kind=kOutput, calls=%fused_computation.27.clone.1 | convolution fusion | flops 45219840 | bytes 3377344 | tf_op jit(solution)/shard_map/while/body/eval_jaxpr/vmap()/dot_general | solution.py:59
  69.6 2.3 fusion.122
  71.9 2.6 fusion.128
  97.7 8.9 %while.27 = (s32[]{:T(128)}, bf16[64,16384]{1,0:T(8,128)(2,1)}, s32[4,2]{0,1:T(2,128)S(1)}, bf16[4,64,512]{2,1,0:T(8,128)(2,1)S(1)}, s32[]{:T(128)}) while((s32[]{:T(128)}, bf16[64,16384]{1,0:T(8,128)(2,1)}, s32[4,2]{0,1:T(2,128)S(1)}, bf16[4,64,512]{2,1,0:T(8,128)(2,1)S(1)}, s32[]{:T(128)}) %tuple.81), condition=%wide.while_cond, body=%wide.while_body.sunk | while | flops 2 | bytes 131177 | solution.py:35
  106.9 2.2 convert_reduce_fusion.2
  109.1 5.4 %fusion.121 = (bf16[4,80,1024]{2,1,0:T(8,128)(2,1)S(1)}, f32[4,80,1024]{2,1,0:T(8,128)}, f32[4,1024,80]{1,2,0:T(8,128)}) fusion(f32[80]{0:T(128)S(1)} %get-tuple-element.726, f32[80,6]{0,1:T(8,128)S(1)} %get-tuple-element.725, f32[4,6,1024]{2,0,1:T(4,128)S(1)} %pad_maximum_fusion.2), kind=kOutput, calls=%fused_computation.27.clone.1 | convolution fusion | flops 45219840 | bytes 3377344 | tf_op jit(solution)/shard_map/while/body/eval_jaxpr/vmap()/dot_general | solution.py:59
  114.5 2.3 fusion.122
  116.8 2.6 fusion.128
  122.0 1.9 dynamic_update_slice.36
  142.6 8.9 %while.27 = (s32[]{:T(128)}, bf16[64,16384]{1,0:T(8,128)(2,1)}, s32[4,2]{0,1:T(2,128)S(1)}, bf16[4,64,512]{2,1,0:T(8,128)(2,1)S(1)}, s32[]{:T(128)}) while((s32[]{:T(128)}, bf16[64,16384]{1,0:T(8,128)(2,1)}, s32[4,2]{0,1:T(2,128)S(1)}, bf16[4,64,512]{2,1,0:T(8,128)(2,1)S(1)}, s32[]{:T(128)}) %tuple.81), condition=%wide.while_cond, body=%wide.while_body.sunk | while | flops 2 | bytes 131177 | solution.py:35
  151.8 2.2 convert_reduce_fusion.2
  154.0 5.4 %fusion.121 = (bf16[4,80,1024]{2,1,0:T(8,128)(2,1)S(1)}, f32[4,80,1024]{2,1,0:T(8,128)}, f32[4,1024,80]{1,2,0:T(8,128)}) fusion(f32[80]{0:T(128)S(1)} %get-tuple-element.726, f32[80,6]{0,1:T(8,128)S(1)} %get-tuple-element.725, f32[4,6,1024]{2,0,1:T(4,128)S(1)} %pad_maximum_fusion.2), kind=kOutput, calls=%fused_computation.27.clone.1 | convolution fusion | flops 45219840 | bytes 3377344 | tf_op jit(solution)/shard_map/while/body/eval_jaxpr/vmap()/dot_general | solution.py:59
  159.4 2.3 fusion.122
  161.7 2.6 fusion.128
  187.4 8.9 %while.27 = (s32[]{:T(128)}, bf16[64,16384]{1,0:T(8,128)(2,1)}, s32[4,2]{0,1:T(2,128)S(1)}, bf16[4,64,512]{2,1,0:T(8,128)(2,1)S(1)}, s32[]{:T(128)}) while((s32[]{:T(128)}, bf16[64,16384]{1,0:T(8,128)(2,1)}, s32[4,2]{0,1:T(2,128)S(1)}, bf16[4,64,512]{2,1,0:T(8,128)(2,1)S(1)}, s32[]{:T(128)}) %tuple.81), condition=%wide.while_cond, body=%wide.while_body.sunk | while | flops 2 | bytes 131177 | solution.py:35
  196.6 2.2 convert_reduce_fusion.2
  198.9 5.4 %fusion.121 = (bf16[4,80,1024]{2,1,0:T(8,128)(2,1)S(1)}, f32[4,80,1024]{2,1,0:T(8,128)}, f32[4,1024,80]{1,2,0:T(8,128)}) fusion(f32[80]{0:T(128)S(1)} %get-tuple-element.726, f32[80,6]{0,1:T(8,128)S(1)} %get-tuple-element.725, f32[4,6,1024]{2,0,1:T(4,128)S(1)} %pad_maximum_fusion.2), kind=kOutput, calls=%fused_computation.27.clone.1 | convolution fusion | flops 45219840 | bytes 3377344 | tf_op jit(solution)/shard_map/while/body/eval_jaxpr/vmap()/dot_general | solution.py:59
  204.2 2.3 fusion.122
  206.6 2.6 fusion.128
  232.3 8.9 %while.27 = (s32[]{:T(128)}, bf16[64,16384]{1,0:T(8,128)(2,1)}, s32[4,2]{0,1:T(2,128)S(1)}, bf16[4,64,512]{2,1,0:T(8,128)(2,1)S(1)}, s32[]{:T(128)}) while((s32[]{:T(128)}, bf16[64,16384]{1,0:T(8,128)(2,1)}, s32[4,2]{0,1:T(2,128)S(1)}, bf16[4,64,512]{2,1,0:T(8,128)(2,1)S(1)}, s32[]{:T(128)}) %tuple.81), condition=%wide.while_cond, body=%wide.while_body.sunk | while | flops 2 | bytes 131177 | solution.py:35
  241.5 2.2 convert_reduce_fusion.2
  243.8 5.4 %fusion.121 = (bf16[4,80,1024]{2,1,0:T(8,128)(2,1)S(1)}, f32[4,80,1024]{2,1,0:T(8,128)}, f32[4,1024,80]{1,2,0:T(8,128)}) fusion(f32[80]{0:T(128)S(1)} %get-tuple-element.726, f32[80,6]{0,1:T(8,128)S(1)} %get-tuple-element.725, f32[4,6,1024]{2,0,1:T(4,128)S(1)} %pad_maximum_fusion.2), kind=kOutput, calls=%fused_computation.27.clone.1 | convolution fusion | flops 45219840 | bytes 3377344 | tf_op jit(solution)/shard_map/while/body/eval_jaxpr/vmap()/dot_general | solution.py:59
  249.1 2.3 fusion.122
  251.5 2.6 fusion.128
  277.2 8.9 %while.27 = (s32[]{:T(128)}, bf16[64,16384]{1,0:T(8,128)(2,1)}, s32[4,2]{0,1:T(2,128)S(1)}, bf16[4,64,512]{2,1,0:T(8,128)(2,1)S(1)}, s32[]{:T(128)}) while((s32[]{:T(128)}, bf16[64,16384]{1,0:T(8,128)(2,1)}, s32[4,2]{0,1:T(2,128)S(1)}, bf16[4,64,512]{2,1,0:T(8,128)(2,1)S(1)}, s32[]{:T(128)}) %tuple.81), condition=%wide.while_cond, body=%wide.while_body.sunk | while | flops 2 | bytes 131177 | solution.py:35
  286.4 2.2 convert_reduce_fusion.2
  288.6 5.4 %fusion.121 = (bf16[4,80,1024]{2,1,0:T(8,128)(2,1)S(1)}, f32[4,80,1024]{2,1,0:T(8,128)}, f32[4,1024,80]{1,2,0:T(8,128)}) fusion(f32[80]{0:T(128)S(1)} %get-tuple-element.726, f32[80,6]{0,1:T(8,128)S(1)} %get-tuple-element.725, f32[4,6,1024]{2,0,1:T(4,128)S(1)} %pad_maximum_fusion.2), kind=kOutput, calls=%fused_computation.27.clone.1 | convolution fusion | flops 45219840 | bytes 3377344 | tf_op jit(solution)/shard_map/while/body/eval_jaxpr/vmap()/dot_general | solution.py:59
  294.0 2.3 fusion.122
  296.3 2.6 fusion.128
  301.5 1.9 dynamic_update_slice.36
  322.1 8.9 %while.27 = (s32[]{:T(128)}, bf16[64,16384]{1,0:T(8,128)(2,1)}, s32[4,2]{0,1:T(2,128)S(1)}, bf16[4,64,512]{2,1,0:T(8,128)(2,1)S(1)}, s32[]{:T(128)}) while((s32[]{:T(128)}, bf16[64,16384]{1,0:T(8,128)(2,1)}, s32[4,2]{0,1:T(2,128)S(1)}, bf16[4,64,512]{2,1,0:T(8,128)(2,1)S(1)}, s32[]{:T(128)}) %tuple.81), condition=%wide.while_cond, body=%wide.while_body.sunk | while | flops 2 | bytes 131177 | solution.py:35
  331.3 2.2 convert_reduce_fusion.2
  333.5 5.4 %fusion.121 = (bf16[4,80,1024]{2,1,0:T(8,128)(2,1)S(1)}, f32[4,80,1024]{2,1,0:T(8,128)}, f32[4,1024,80]{1,2,0:T(8,128)}) fusion(f32[80]{0:T(128)S(1)} %get-tuple-element.726, f32[80,6]{0,1:T(8,128)S(1)} %get-tuple-element.725, f32[4,6,1024]{2,0,1:T(4,128)S(1)} %pad_maximum_fusion.2), kind=kOutput, calls=%fused_computation.27.clone.1 | convolution fusion | flops 45219840 | bytes 3377344 | tf_op jit(solution)/shard_map/while/body/eval_jaxpr/vmap()/dot_general | solution.py:59
  338.9 2.3 fusion.122
  341.2 2.6 fusion.128
  352.1 1.9 dynamic_update_slice.38
  366.9 8.9 %while.27 = (s32[]{:T(128)}, bf16[64,16384]{1,0:T(8,128)(2,1)}, s32[4,2]{0,1:T(2,128)S(1)}, bf16[4,64,512]{2,1,0:T(8,128)(2,1)S(1)}, s32[]{:T(128)}) while((s32[]{:T(128)}, bf16[64,16384]{1,0:T(8,128)(2,1)}, s32[4,2]{0,1:T(2,128)S(1)}, bf16[4,64,512]{2,1,0:T(8,128)(2,1)S(1)}, s32[]{:T(128)}) %tuple.81), condition=%wide.while_cond, body=%wide.while_body.sunk | while | flops 2 | bytes 131177 | solution.py:35
  376.1 2.2 convert_reduce_fusion.2
  378.4 5.4 %fusion.121 = (bf16[4,80,1024]{2,1,0:T(8,128)(2,1)S(1)}, f32[4,80,1024]{2,1,0:T(8,128)}, f32[4,1024,80]{1,2,0:T(8,128)}) fusion(f32[80]{0:T(128)S(1)} %get-tuple-element.726, f32[80,6]{0,1:T(8,128)S(1)} %get-tuple-element.725, f32[4,6,1024]{2,0,1:T(4,128)S(1)} %pad_maximum_fusion.2), kind=kOutput, calls=%fused_computation.27.clone.1 | convolution fusion | flops 45219840 | bytes 3377344 | tf_op jit(solution)/shard_map/while/body/eval_jaxpr/vmap()/dot_general | solution.py:59
  383.7 2.3 fusion.122
  386.0 2.6 fusion.128
  401.8 40.1 %all-reduce.1 = (f32[80,6]{0,1:T(8,128)S(1)}, f32[80]{0:T(128)S(1)}, f32[64,80]{1,0:T(8,128)S(1)}, f32[64]{0:T(128)S(1)}) all-reduce(f32[80,6]{0,1:T(8,128)S(1)} %get-tuple-element.285, f32[80]{0:T(128)S(1)} %get-tuple-element.286, f32[64,80]{1,0:T(8,128)S(1)} %get-tuple-element.287, ...), channel_id=1, replica_groups=mesh['pb'=8,'ga'=4] {'pb','ga'}, use_global_device_ids=true, to_apply=%region_5.6 | all-reduce | flops 5744 | bytes 45952 | tf_op jit(solution)/shard_map/psum | solution.py:120
  444.1 9.4 %reduce-scatter.2.cloned.1.call-done = f32[64,2048]{1,0:T(8,128)} async-done(((f32[64,16384]{1,0:T(8,128)}), f32[64,2048]{1,0:T(8,128)}) %reduce-scatter.2.cloned.1.call-update) | async-done | bytes 524304 | tf_op jit(solution)/shard_map/reduce_scatter | solution.py:119
  (398 shorter events, 198.3 us)
Async XLA Ops:
  7.2 33.2 %all-gather.2.cloned.1.call-start = ((), (), s32[]{:S(2)}) async-start(), calls=%async_computation.1 | async-start | bytes 2359296 | tf_op jit(solution)/shard_map/all_gather | solution.py:21
  7.9 445.6 %reduce-scatter.2.cloned.1.call-start = ((), (), s32[]{:S(2)}) async-start(), calls=%async_computation.2 | async-start | bytes 4718592 | tf_op jit(solution)/shard_map/reduce_scatter | solution.py:119
  40.4 2.3 copy-start.2
  40.4 2.3 copy-start.3
  40.4 2.3 copy-start.4
  40.4 2.3 copy-start.5
  42.7 19.1 %copy-start = (bf16[8,4,64,128]{3,1,0,2:T(4,128)(2,1)}, bf16[8,4,64,128]{3,1,0,2:T(4,128)(2,1)S(1)}, u32[]{:S(2)}) copy-start(bf16[8,4,64,128]{3,1,0,2:T(4,128)(2,1)S(1)} %get-tuple-element.729) | copy-start | bytes 1572868 | tf_op jit(solution)/shard_map/while
  76.0 11.6 %copy-start.1 = (bf16[8,4,64,128]{3,1,0,2:T(4,128)(2,1)S(1)}, bf16[8,4,64,128]{3,1,0,2:T(4,128)(2,1)}, u32[]{:S(2)}) copy-start(bf16[8,4,64,128]{3,1,0,2:T(4,128)(2,1)} %copy-done) | copy-start | bytes 1572868 | tf_op jit(solution)/shard_map/while
  87.6 19.0 %copy-start = (bf16[8,4,64,128]{3,1,0,2:T(4,128)(2,1)}, bf16[8,4,64,128]{3,1,0,2:T(4,128)(2,1)S(1)}, u32[]{:S(2)}) copy-start(bf16[8,4,64,128]{3,1,0,2:T(4,128)(2,1)S(1)} %get-tuple-element.729) | copy-start | bytes 1572868 | tf_op jit(solution)/shard_map/while
  120.9 11.6 %copy-start.1 = (bf16[8,4,64,128]{3,1,0,2:T(4,128)(2,1)S(1)}, bf16[8,4,64,128]{3,1,0,2:T(4,128)(2,1)}, u32[]{:S(2)}) copy-start(bf16[8,4,64,128]{3,1,0,2:T(4,128)(2,1)} %copy-done) | copy-start | bytes 1572868 | tf_op jit(solution)/shard_map/while
  132.5 19.0 %copy-start = (bf16[8,4,64,128]{3,1,0,2:T(4,128)(2,1)}, bf16[8,4,64,128]{3,1,0,2:T(4,128)(2,1)S(1)}, u32[]{:S(2)}) copy-start(bf16[8,4,64,128]{3,1,0,2:T(4,128)(2,1)S(1)} %get-tuple-element.729) | copy-start | bytes 1572868 | tf_op jit(solution)/shard_map/while
  165.8 11.6 %copy-start.1 = (bf16[8,4,64,128]{3,1,0,2:T(4,128)(2,1)S(1)}, bf16[8,4,64,128]{3,1,0,2:T(4,128)(2,1)}, u32[]{:S(2)}) copy-start(bf16[8,4,64,128]{3,1,0,2:T(4,128)(2,1)} %copy-done) | copy-start | bytes 1572868 | tf_op jit(solution)/shard_map/while
  177.3 19.0 %copy-start = (bf16[8,4,64,128]{3,1,0,2:T(4,128)(2,1)}, bf16[8,4,64,128]{3,1,0,2:T(4,128)(2,1)S(1)}, u32[]{:S(2)}) copy-start(bf16[8,4,64,128]{3,1,0,2:T(4,128)(2,1)S(1)} %get-tuple-element.729) | copy-start | bytes 1572868 | tf_op jit(solution)/shard_map/while
  210.6 11.6 %copy-start.1 = (bf16[8,4,64,128]{3,1,0,2:T(4,128)(2,1)S(1)}, bf16[8,4,64,128]{3,1,0,2:T(4,128)(2,1)}, u32[]{:S(2)}) copy-start(bf16[8,4,64,128]{3,1,0,2:T(4,128)(2,1)} %copy-done) | copy-start | bytes 1572868 | tf_op jit(solution)/shard_map/while
  222.2 19.0 %copy-start = (bf16[8,4,64,128]{3,1,0,2:T(4,128)(2,1)}, bf16[8,4,64,128]{3,1,0,2:T(4,128)(2,1)S(1)}, u32[]{:S(2)}) copy-start(bf16[8,4,64,128]{3,1,0,2:T(4,128)(2,1)S(1)} %get-tuple-element.729) | copy-start | bytes 1572868 | tf_op jit(solution)/shard_map/while
  255.5 11.6 %copy-start.1 = (bf16[8,4,64,128]{3,1,0,2:T(4,128)(2,1)S(1)}, bf16[8,4,64,128]{3,1,0,2:T(4,128)(2,1)}, u32[]{:S(2)}) copy-start(bf16[8,4,64,128]{3,1,0,2:T(4,128)(2,1)} %copy-done) | copy-start | bytes 1572868 | tf_op jit(solution)/shard_map/while
  267.1 19.0 %copy-start = (bf16[8,4,64,128]{3,1,0,2:T(4,128)(2,1)}, bf16[8,4,64,128]{3,1,0,2:T(4,128)(2,1)S(1)}, u32[]{:S(2)}) copy-start(bf16[8,4,64,128]{3,1,0,2:T(4,128)(2,1)S(1)} %get-tuple-element.729) | copy-start | bytes 1572868 | tf_op jit(solution)/shard_map/while
  300.4 11.6 %copy-start.1 = (bf16[8,4,64,128]{3,1,0,2:T(4,128)(2,1)S(1)}, bf16[8,4,64,128]{3,1,0,2:T(4,128)(2,1)}, u32[]{:S(2)}) copy-start(bf16[8,4,64,128]{3,1,0,2:T(4,128)(2,1)} %copy-done) | copy-start | bytes 1572868 | tf_op jit(solution)/shard_map/while
  312.0 19.0 %copy-start = (bf16[8,4,64,128]{3,1,0,2:T(4,128)(2,1)}, bf16[8,4,64,128]{3,1,0,2:T(4,128)(2,1)S(1)}, u32[]{:S(2)}) copy-start(bf16[8,4,64,128]{3,1,0,2:T(4,128)(2,1)S(1)} %get-tuple-element.729) | copy-start | bytes 1572868 | tf_op jit(solution)/shard_map/while
  345.3 11.6 %copy-start.1 = (bf16[8,4,64,128]{3,1,0,2:T(4,128)(2,1)S(1)}, bf16[8,4,64,128]{3,1,0,2:T(4,128)(2,1)}, u32[]{:S(2)}) copy-start(bf16[8,4,64,128]{3,1,0,2:T(4,128)(2,1)} %copy-done) | copy-start | bytes 1572868 | tf_op jit(solution)/shard_map/while
  356.8 19.0 %copy-start = (bf16[8,4,64,128]{3,1,0,2:T(4,128)(2,1)}, bf16[8,4,64,128]{3,1,0,2:T(4,128)(2,1)S(1)}, u32[]{:S(2)}) copy-start(bf16[8,4,64,128]{3,1,0,2:T(4,128)(2,1)S(1)} %get-tuple-element.729) | copy-start | bytes 1572868 | tf_op jit(solution)/shard_map/while
  390.1 11.6 %copy-start.1 = (bf16[8,4,64,128]{3,1,0,2:T(4,128)(2,1)S(1)}, bf16[8,4,64,128]{3,1,0,2:T(4,128)(2,1)}, u32[]{:S(2)}) copy-start(bf16[8,4,64,128]{3,1,0,2:T(4,128)(2,1)} %copy-done) | copy-start | bytes 1572868 | tf_op jit(solution)/shard_map/while
Sparse Core Ops, SparseCore 0:
  9.9 30.4 all-gather.1
  401.9 51.5 reduce-scatter.1
where the time goes:
time: 465 us; the launch traced here: 460 us
  local copies, waits for them, and re-layouts  149 us (32%)
  matrix products  112 us (24%)
  loops' own time  62.8 us (14%)
  other arithmetic  44.2 us (10%)
  blocking collectives  40.1 us (9%)
  waiting for transfers between devices  38.3 us (8%)
  between operations  14.1 us (3%)
    gather x96, local copies, waits for them, and re-layouts  70.8 us
    another operation x1, loops' own time, shards(): lax.scan(advance, (start_grid, start_totals), inputs_all)  62.1 us
    dynamic_update_slice x32, local copies, waits for them, and re-layouts, advance(): lax.dynamic_update_slice_in_dim(partial_grad, current + results[0][number...  59.4 us
    dot_general x8, matrix products, tile_work(): jnp.dot(w_in, features_in, precision=lax.Precision.HIGHEST, preferred_ele...  43 us
    psum x1, blocking collectives, shards(): sums = lax.psum((totals[0], totals[1], totals[2], totals[3]), ('pb', 'ga'))  40.1 us
    add x32, other arithmetic, advance(): current + results[0][number]  32.9 us
    all_gather x1, waiting for transfers between devices, shards(): slab_feats = lax.all_gather(latent, 'pb', axis=2, tiled=True)[0]  28.2 us
    dot_general x8, matrix products, tile_work(): lax.dot_general(w_out, grad_kernel, (((0,), (0,)), ((), ())), preferred_e...  20.4 us
  transfers between devices with their start and end apart: 2, of which 2 were waited for; matrix products, arithmetic and copies ran while one was open for 1% of the time, Pallas kernels for 0%

commit v1 on v0

v1 whole, which is shorter than its diff:
```python
import functools
import math

import jax
import jax.numpy as jnp
from jax import lax
from jax.experimental import pallas as pl
from jax.experimental.pallas import tpu as pltpu
from jax.sharding import PartitionSpec as P


TILE = 128
WIN = 512
GX = 64
ZS = 4
LANES = 128
CHUNK = 256
REACH = WIN + LANES
LANE_BIT = 9
SHIFT_BIT = 16
LIVE = 1 << 24
HALF_ROOT = 0.7071067811865476
DENSITY = 0.3989422804014327


def compact_kernel(slots, slab_ref, slabs_ref, rels_ref, out_ref):
    tiles = slabs_ref.shape[1] // TILE
    here = slab_ref[0]
    slabs = jnp.concatenate([slabs_ref[:, t * TILE:(t + 1) * TILE] for t in range(tiles)], 0)
    rels = jnp.concatenate([rels_ref[:, t * TILE:(t + 1) * TILE] for t in range(tiles)], 0)
    rows = tiles * slots
    live = slabs == here
    lane = lax.broadcasted_iota(jnp.int32, (rows, TILE), 1)
    upper = (
        lax.broadcasted_iota(jnp.int32, (TILE, TILE), 0)
        <= lax.broadcasted_iota(jnp.int32, (TILE, TILE), 1)
    ).astype(jnp.float32).astype(jnp.bfloat16)
    flags = live.astype(jnp.float32).astype(jnp.bfloat16)
    prefix = jnp.dot(flags, upper, preferred_element_type=jnp.float32)
    every = jnp.ones((TILE, TILE), jnp.bfloat16)
    totals = jnp.dot(flags, every, preferred_element_type=jnp.float32)
    row_a = lax.broadcasted_iota(jnp.int32, (rows, rows), 0)
    row_b = lax.broadcasted_iota(jnp.int32, (rows, rows), 1)
    before = ((row_a // slots == row_b // slots) & (row_b < row_a)).astype(jnp.float32).astype(jnp.bfloat16)
    starts = jnp.dot(before, totals.astype(jnp.bfloat16), preferred_element_type=jnp.float32)
    starts = starts.astype(jnp.int32)
    totals = totals.astype(jnp.int32)
    move_by = lane - prefix.astype(jnp.int32) + 1
    held = jnp.where(live, rels + lane * (1 << LANE_BIT) + move_by * (1 << SHIFT_BIT) + LIVE, 0)
    for bit in range(7):
        step = 1 << bit
        flag = 1 << (SHIFT_BIT + bit)
        come = pltpu.roll(held, TILE - step, 1)
        held = jnp.where(come & flag != 0, come, jnp.where(held & flag != 0, 0, held))
    for t in range(tiles):
        part = held[t * slots:(t + 1) * slots]
        start = starts[t * slots:(t + 1) * slots]
        total = totals[t * slots:(t + 1) * slots]
        spots = lax.broadcasted_iota(jnp.int32, (slots, TILE), 1)
        lines = []
        for r in range(slots):
            local = spots + r * TILE - start
            own = (local >= 0) & (local < total)
            got = jnp.take_along_axis(part, jnp.clip(local, 0, TILE - 1), axis=1)
            lines.append(jnp.sum(jnp.where(own, got, 0), axis=0, keepdims=True))
        out_ref[t] = jnp.concatenate(lines, 0)


def erf_of(x):
    return lax.erf(x)


def entry_values(chunk, slab, anchor, base, meta, points, cot, win_ref):
    lines = [meta[pl.ds(chunk * 2 + half, 1), :] for half in range(2)]
    packed = jnp.concatenate(lines, 1)
    rel = packed & (WIN - 1)
    picks = [(line >> LANE_BIT) & (TILE - 1) for line in lines]
    valid = packed >= LIVE
    cell = rel + anchor
    spot = jnp.where(valid, cell - base, -1)
    coords = jnp.concatenate(
        [jnp.take_along_axis(points, jnp.broadcast_to(p, points.shape), axis=1) for p in picks], 1
    )
    cots = jnp.concatenate(
        [jnp.take_along_axis(cot, jnp.broadcast_to(p, cot.shape), axis=1) for p in picks], 1
    )
    along_x = ((cell >> 8).astype(jnp.float32) + 0.5) / GX
    along_y = (((cell >> 2) & (GX - 1)).astype(jnp.float32) + 0.5) / GX
    along_z = (((cell & (ZS - 1)) + slab * ZS).astype(jnp.float32) + 0.5) / GX
    inputs = [coords[0:1], coords[1:2], coords[2:3], along_x, along_y, along_z]
    preact = jnp.concatenate([win_ref[6]] * 2, 1)
    for number, line in enumerate(inputs):
        preact = preact + jnp.concatenate([win_ref[number]] * 2, 1) * line
    hot = lax.broadcasted_iota(jnp.int32, (REACH, CHUNK), 0) == spot
    hot = hot.astype(jnp.float32).astype(jnp.bfloat16)
    return preact, inputs, cots, hot


def tile_place(offsets_ref, tile, cells):
    anchor = offsets_ref[tile]
    base = jnp.minimum(anchor // LANES * LANES, cells - REACH)
    return anchor, pl.multiple_of(base, LANES)


def mask_of(place, bits):
    mask = 0
    for number, bit in enumerate(reversed(bits)):
        if place >> number & 1:
            mask |= bit
    return mask


def scatter_kernel(group, orders, offsets_ref, chunks_ref, slab_ref, meta_ref, points_ref, cot_ref,
                   win_ref, wout_ref, bout_ref, *refs):
    out_refs, grid_ref = refs[:-1], refs[-1]
    step = pl.program_id(0)
    cells = grid_ref.shape[1]
    slab = slab_ref[0]

    @pl.when(step == 0)
    def _():
        grid_ref[...] = jnp.zeros_like(grid_ref)

    most = chunks_ref[step * group]
    for g in range(1, group):
        most = jnp.maximum(most, chunks_ref[step * group + g])

    def body(chunk, carry):
        updates = []
        for g in range(group):
            anchor, base = tile_place(offsets_ref, step * group + g, cells)
            columns = slice(g * TILE, (g + 1) * TILE)
            cot = cot_ref[:, columns].astype(jnp.float32)
            preact, _, cots, hot = entry_values(
                chunk, slab, anchor, base, meta_ref.at[g], points_ref[:, columns], cot, win_ref)
            hidden = (0.5 * preact * (1.0 + erf_of(preact * HALF_ROOT))).astype(jnp.bfloat16)
            kernel = jnp.dot(wout_ref[...], hidden, preferred_element_type=jnp.float32)
            kernel = kernel + jnp.concatenate([bout_ref[...]] * 2, 1)
            grad_cell = (kernel * cots).astype(jnp.bfloat16)
            updates.append((base, lax.dot_general(
                grad_cell, hot, (((1,), (1,)), ((), ())), preferred_element_type=jnp.float32)))
        for base, update in updates:
            grid_ref[:, pl.ds(base, REACH)] += update
        return carry

    lax.fori_loop(0, most, body, 0)

    @pl.when(step == pl.num_programs(0) - 1)
    def _():
        half, own = out_refs[0].shape[1:]
        for number, (out_ref, bits) in enumerate(zip(out_refs, orders)):
            for place in range(out_ref.shape[0]):
                owner = slab_ref[1] ^ mask_of(place, bits)
                columns = pl.ds(pl.multiple_of(owner * own, own), own)
                out_ref[place] = grid_ref[pl.ds(number * half, half), columns].astype(out_ref.dtype)


def weight_kernel(group, offsets_ref, chunks_ref, slab_ref, meta_ref, points_ref, cot_ref,
                  win_ref, wout_t_ref, latent_ref, out_ref, slab_feats, total_ref):
    step = pl.program_id(0)
    cells = slab_feats.shape[1]
    slab = slab_ref[0]
    channels = cot_ref.shape[0]
    units = wout_t_ref.shape[0]

    @pl.when(step == 0)
    def _():
        total_ref[...] = jnp.zeros_like(total_ref)
        own = latent_ref.shape[2]
        for owner in range(latent_ref.shape[0]):
            slab_feats[:, owner * own:(owner + 1) * own] = latent_ref[owner]

    most = chunks_ref[step * group]
    for g in range(1, group):
        most = jnp.maximum(most, chunks_ref[step * group + g])

    def body(chunk, carry):
        total = None
        for g in range(group):
            anchor, base = tile_place(offsets_ref, step * group + g, cells)
            columns = slice(g * TILE, (g + 1) * TILE)
            cot = cot_ref[:, columns].astype(jnp.float32)
            preact, inputs, cots, hot = entry_values(
                chunk, slab, anchor, base, meta_ref.at[g], points_ref[:, columns], cot, win_ref)
            window = slab_feats[:, pl.ds(base, REACH)]
            feats = jnp.dot(window, hot, preferred_element_type=jnp.float32)
            grad_kernel = (feats * cots).astype(jnp.bfloat16)
            cdf = 0.5 * (1.0 + erf_of(preact * HALF_ROOT))
            hidden = (preact * cdf).astype(jnp.bfloat16)
            slope = cdf + preact * (DENSITY * jnp.exp(-0.5 * preact * preact))
            grad_hidden = jnp.dot(wout_t_ref[...], grad_kernel, preferred_element_type=jnp.float32)
            grad_pre = grad_hidden * slope
            pre_hi = grad_pre.astype(jnp.bfloat16)
            pre_lo = (grad_pre - pre_hi.astype(jnp.float32)).astype(jnp.bfloat16)
            ones = jnp.ones((1, CHUNK), jnp.float32)
            lines = jnp.concatenate(inputs + [ones, ones * 0.0], 0)
            in_hi = lines.astype(jnp.bfloat16).astype(jnp.float32)
            both = jnp.concatenate([in_hi, lines - in_hi], 0).astype(jnp.bfloat16)
            left = jnp.concatenate([grad_kernel, pre_hi, pre_lo], 0)
            right = jnp.concatenate([hidden, both], 0)
            update = lax.dot_general(
                left, right, (((1,), (1,)), ((), ())), preferred_element_type=jnp.float32)
            total = update if total is None else total + update
        total_ref[...] += total
        return carry

    lax.fori_loop(0, most, body, 0)

    @pl.when(step == pl.num_programs(0) - 1)
    def _():
        out_ref[0:channels] = total_ref[0:channels]
        out_ref[channels:channels + units] = (
            total_ref[channels:channels + units] + total_ref[channels + units:channels + 2 * units])


def exchange(values, axis, bit):
    size = lax.axis_size(axis)
    return lax.ppermute(values, axis, [(i, i ^ bit) for i in range(size)])


def butterfly(values, axis):
    size = lax.axis_size(axis)
    if size & (size - 1):
        return lax.psum(values, axis)
    bit = 1
    while bit < size:
        values = values + exchange(values, axis, bit)
        bit *= 2
    return values


def halve(values, bits):
    for number, bit in enumerate(bits):
        middle = values.shape[0] // 2
        come = exchange(values[middle:], "pb", bit)
        values = values[:middle].astype(jnp.float32) + come.astype(jnp.float32)
        if number < len(bits) - 1:
            values = values.astype(jnp.bfloat16)
    return values[0]


def parts(query_points, cotangent, slab_ids, rel_cells, offsets, latent, w_in, b_in, w_out, b_out):
    channels, own_cells = latent.shape[1:]
    owners = lax.axis_size("pb")
    slots, queries_dev = slab_ids.shape
    units = w_in.shape[0]
    tiles = queries_dev // TILE
    group = math.gcd(tiles, 2)
    cells = owners * own_cells
    slab = jnp.stack([lax.axis_index("ga"), lax.axis_index("pb")]).astype(jnp.int32)
    bits = [1 << number for number in range(owners.bit_length() - 1)]
    assert owners == 1 << len(bits)
    orders = [bits, bits[:1] + bits[:0:-1]]

    gathered = lax.all_gather(latent[0], "pb", axis=0)

    counts = jnp.sum((slab_ids == slab[0]).astype(jnp.int32).reshape(slots, tiles, TILE), (0, 2))
    chunks = (counts + CHUNK - 1) // CHUNK
    anchors = offsets[0]
    smem = pl.BlockSpec(memory_space=pltpu.SMEM)
    vmem = pl.BlockSpec(memory_space=pltpu.VMEM)
    meta = pl.pallas_call(
        functools.partial(compact_kernel, slots),
        out_shape=jax.ShapeDtypeStruct((tiles, slots, TILE), jnp.int32),
        in_specs=[smem, vmem, vmem],
        out_specs=vmem,
        name="compact",
        cost_estimate=pl.CostEstimate(flops=10**8, bytes_accessed=queries_dev * slots * 12, transcendentals=0),
    )(slab, slab_ids, rel_cells)

    points = jnp.pad(query_points, ((0, 5), (0, 0)))
    w_lines = jnp.concatenate([w_in.T, b_in[None]], 0)
    w_lines = jnp.broadcast_to(w_lines[:, :, None], (7, units, LANES))
    b_lines = jnp.broadcast_to(b_out[:, None], (channels, LANES))

    def whole(shape):
        return pl.BlockSpec(shape, lambda i, *_: (0,) * len(shape))

    def by_tile(rows):
        return pl.BlockSpec((rows, group * TILE), lambda i, *_: (0, i))

    meta_spec = pl.BlockSpec((group, slots, TILE), lambda i, *_: (i, 0, 0))
    shared = [meta_spec, by_tile(8), by_tile(channels), whole(w_lines.shape)]
    work = 4 * channels * REACH * tiles * CHUNK * 4
    params = pltpu.CompilerParams(
        dimension_semantics=("arbitrary",), vmem_limit_bytes=40 * 1024 * 1024)
    scatter_call = pl.pallas_call(
        functools.partial(scatter_kernel, group, orders),
        out_shape=[jax.ShapeDtypeStruct((owners, channels // 2, own_cells), jnp.bfloat16)] * 2,
        grid_spec=pltpu.PrefetchScalarGridSpec(
            num_scalar_prefetch=3,
            grid=(tiles // group,),
            in_specs=shared + [whole(w_out.shape), whole(b_lines.shape)],
            out_specs=[whole((owners, channels // 2, own_cells))] * 2,
            scratch_shapes=[pltpu.VMEM((channels, cells), jnp.float32)],
        ),
        compiler_params=params,
        name="scatter",
        cost_estimate=pl.CostEstimate(flops=work, bytes_accessed=10**7, transcendentals=0),
    )
    partial_grad = scatter_call(
        anchors, chunks, slab, meta, points, cotangent, w_lines, w_out, b_lines)

    owned = jnp.concatenate([halve(p, o) for p, o in zip(partial_grad, orders)], 0)

    weights_call = pl.pallas_call(
        functools.partial(weight_kernel, group),
        out_shape=jax.ShapeDtypeStruct((channels + units, units + 16), jnp.float32),
        grid_spec=pltpu.PrefetchScalarGridSpec(
            num_scalar_prefetch=3,
            grid=(tiles // group,),
            in_specs=shared + [whole((units, channels)), whole(gathered.shape)],
            out_specs=whole((channels + units, units + 16)),
            scratch_shapes=[
                pltpu.VMEM((channels, cells), jnp.bfloat16),
                pltpu.VMEM((channels + 2 * units, units + 16), jnp.float32),
            ],
        ),
        compiler_params=params,
        name="weights",
        cost_estimate=pl.CostEstimate(flops=work, bytes_accessed=10**7, transcendentals=0),
    )
    sums = weights_call(
        anchors, chunks, slab, meta, points, cotangent, w_lines, w_out.T, gathered)

    scale = float(queries_dev * owners) ** (-0.5)
    sums = butterfly(butterfly(sums, "pb"), "ga") * scale
    ins = sums[channels:, units:units + 8] + sums[channels:, units + 8:units + 16]
    return (
        owned.astype(jnp.float32)[None],
        ins[:, :6],
        ins[:, 6],
        sums[:channels, :units],
        sums[:channels, units + 6],
    )


def solution(mesh):
    return jax.shard_map(
        parts,
        mesh=mesh,
        in_specs=(
            P(None, "pb"),
            P(None, "pb"),
            P(None, "pb"),
            P(None, "pb"),
            P("ga", "pb"),
            P("ga", None, "pb"),
            P(),
            P(),
            P(),
            P(),
        ),
        out_specs=(P("ga", None, "pb"), P(), P(), P(), P()),
        check_vma=False,
    )
```

time: 465 us -> 87 us (0.19)
  local copies, waits for them, and re-layouts: 149 us -> 12.6 us
  matrix products: 112 us -> 0 us
  loops' own time: 62.8 us -> 0 us
  blocking collectives: 40.1 us -> 0 us
  other arithmetic: 44.2 us -> 5.86 us
  Pallas kernels: 0 us -> 27.1 us
  waiting for transfers between devices: 38.3 us -> 12.3 us
  starting transfers between devices: 0.08 us -> 14.4 us
    dot_general x48 -> x0, matrix products: 112 us -> none  [the longest x8 43 us: tile_work(): jnp.dot(w_in, features_in, precision=lax.Precision.HIGHEST, preferred_ele...]
    gather x96 -> x0, local copies, waits for them, and re-layouts: 70.8 us -> none
    another operation x9 -> x0, loops' own time: 62.8 us -> none  [the longest x1 62.1 us: shards(): lax.scan(advance, (start_grid, start_totals), inputs_all)]
    dynamic_update_slice x32 -> x0, local copies, waits for them, and re-layouts: 59.4 us -> none  [advance(): lax.dynamic_update_slice_in_dim(partial_grad, current + results[0][number...]
    psum x1 -> x0, blocking collectives: 40.1 us -> none  [shards(): sums = lax.psum((totals[0], totals[1], totals[2], totals[3]), ('pb', 'ga'))]
    add x48 -> x5, other arithmetic: 33.1 us -> 0.13 us  [the longest x1 0.08 us: parts(): sums[channels:, units:units + 8] + sums[channels:, units + 8:units + 16]]
    all_gather x1, waiting for transfers between devices: 28.2 us -> 0.01 us  [parts(): gathered = lax.all_gather(latent[0], 'pb', axis=0)]
    pallas_call x0 -> x3, Pallas kernels: none -> 27.1 us  [the longest x1 13.5 us: parts(): weights_call(anchors, chunks, slab, meta, points, cotangent, w_lines, w_o...]
  transfers between devices with their start and end apart: 2 -> 12, of which waited for: 2 -> 5; matrix products, arithmetic and copies ran while one was open for 1% -> 12% of each run, Pallas kernels for 0% -> 31%
where the time goes in v1:
time: 87 us; the launch traced here: 86.5 us
  Pallas kernels  27.1 us (31%)
  starting transfers between devices  14.4 us (17%)
  between operations  14.2 us (16%)
  local copies, waits for them, and re-layouts  12.6 us (14%)
  waiting for transfers between devices  12.3 us (14%)
  other arithmetic  5.86 us (7%)
    ppermute x11, starting transfers between devices, exchange(): return lax.ppermute(values, axis, [(i, i ^ bit) for i in range(size)])  14.4 us
    pallas_call x1, Pallas kernels, parts(): weights_call(anchors, chunks, slab, meta, points, cotangent, w_lines, w_o...  13.5 us
    ppermute x11, waiting for transfers between devices, exchange(): return lax.ppermute(values, axis, [(i, i ^ bit) for i in range(size)])  11.6 us
    pallas_call x1, Pallas kernels, parts(): scatter_call(anchors, chunks, slab, meta, points, cotangent, w_lines, w_o...  10.6 us
    unnamed x28, local copies, waits for them, and re-layouts  6.36 us
    pallas_call x1, Pallas kernels, parts(): pl.pallas_call(functools.partial(compact_kernel, slots), out_shape=jax.Sh...  3.08 us
    slice x6, local copies, waits for them, and re-layouts, halve(): come = exchange(values[middle:], 'pb', bit)  2.49 us
    convert_element_type x4, other arithmetic, halve(): values = values.astype(jnp.bfloat16)  2.46 us
  transfers between devices with their start and end apart: 12, of which 5 were waited for; matrix products, arithmetic and copies ran while one was open for 12% of the time, Pallas kernels for 31%

profile of v1, /device:TPU:0, one launch (start us, length us, event | category | flops | bytes accessed | tf_op | source)
XLA Modules:
  0.0 86.5 jit_solution(8949345103879287450)
XLA Ops:
  7.2 0.0 all-gather.2.cloned.1.call-start
  7.2 0.7 all-gather.2.cloned.1.call-update
  7.9 0.9 pad.4.points_ref
  8.8 0.6 pad_add_fusion.slab_ref
  9.3 3.1 %compact.1.meta_ref = s32[32,8,128]{2,1,0:T(8,128)} custom-call(s32[2]{0:T(128)} %pad_add_fusion.slab_ref, s32[8,4096]{1,0:T(8,128)} %slabs_ref.1, s32[8,4096]{1,0:T(8,128)} %rels_ref.1), custom_call_target="tpu_custom_call" | custom-call | flops 100000000 | bytes 393216 | tf_op jit(solution)/shard_map/compact/pallas_call | solution.py:262
  12.4 0.7 pad_maximum_fusion
  13.1 0.9 %convert_reduce_fusion = s32[4096]{0:T(1024)S(1)} fusion(s32[8,4096]{1,0:T(8,128)} %slabs_ref.1, s32[]{:T(128)} %axis_index.22), kind=kLoop, calls=%fused_computation.7 | loop fusion | flops 94208 | bytes 147460 | tf_op jit(solution)/shard_map/reduce_sum | solution.py:257
  14.1 0.1 bitcast_reduce_fusion
  14.2 0.1 broadcast_in_dim.9.win_ref
  14.4 0.7 broadcast_in_dim.20.bout_ref
  15.1 0.9 %copy-done = s32[32,8,128]{2,1,0:T(8,128)S(1)} copy-done((s32[32,8,128]{2,1,0:T(8,128)S(1)}, s32[32,8,128]{2,1,0:T(8,128)}, u32[]{:S(2)}) %copy-start) | copy-done | bytes 131096
  16.0 0.7 copy-done.2
  16.7 0.7 copy-done.4
  17.4 1.0 %copy-done.7 = bf16[64,4096]{1,0:T(8,128)(2,1)S(1)} copy-done((bf16[64,4096]{1,0:T(8,128)(2,1)S(1)}, bf16[64,4096]{1,0:T(8,128)(2,1)}, u32[]{:S(2)}) %copy-start.7) | copy-done | bytes 524312
  18.4 0.7 copy-done.9
  19.1 10.6 %scatter.1 = (bf16[8,32,2048]{2,1,0:T(8,128)(2,1)S(1)}, bf16[8,32,2048]{2,1,0:T(8,128)(2,1)S(1)}) custom-call(s32[32]{0:T(128)S(1)} %bitcast.16, s32[32]{0:T(128)S(1)} %and_select_fusion.chunks_ref, s32[2]{0:T(128)S(1)} %copy-done.4, s32[32,8,128]{2,1,0:T(8,128)S(1)} %copy-done, f32[8,4096]{1,0:T(8,128)S(1)} %pad.4.points_ref, ...), custom_call_target="tpu_custom_call" | custom-call | flops 5368709120 | bytes 10000000 | tf_op jit(solution)/shard_map/scatter/pallas_call | solution.py:301
  29.7 0.9 slice.55
  30.5 0.5 collective-permute-start
  31.0 0.8 slice.61
  31.8 0.0 collective-permute-start.3
  31.9 0.1 copy.21
  32.0 1.0 %collective-permute-done = bf16[4,32,2048]{2,1,0:T(8,128)(2,1)} collective-permute-done((bf16[4,32,2048]{2,1,0:T(8,128)(2,1)}, bf16[4,32,2048]{2,1,0:T(8,128)(2,1)}, u32[]{:S(2)}, u32[]{:S(2)}) %collective-permute-start) | collective-permute-done | bytes 524320 | tf_op jit(solution)/shard_map/ppermute | solution.py:218
  33.0 1.2 %add_convert_fusion.1 = bf16[4,32,2048]{2,1,0:T(8,128)(2,1)S(1)} fusion(bf16[4,32,2048]{2,1,0:T(8,128)(2,1)} %collective-permute-done, bf16[8,32,2048]{2,1,0:T(8,128)(2,1)S(1)} %get-tuple-element.7), kind=kLoop, calls=%fused_computation.1 | loop fusion | flops 1048576 | bytes 1572864 | tf_op jit(solution)/shard_map/convert_element_type | solution.py:238
  34.1 0.8 slice.73
  34.9 2.8 %collective-permute-start.1 = (bf16[2,32,2048]{2,1,0:T(8,128)(2,1)}, bf16[2,32,2048]{2,1,0:T(8,128)(2,1)S(1)}, u32[]{:S(2)}, u32[]{:S(2)}) collective-permute-start(bf16[2,32,2048]{2,1,0:T(8,128)(2,1)} %slice.73), channel_id=1, source_target_pairs={{0,8},{4,12},{8,0},{12,4},{16,24},{20,28},{24,16},{28,20},{1,9},{5... | collective-permute-start | bytes 786440 | tf_op jit(solution)/shard_map/ppermute | solution.py:218
  37.7 1.2 %add_convert_fusion = bf16[4,32,2048]{2,1,0:T(8,128)(2,1)S(1)} fusion(bf16[4,32,2048]{2,1,0:T(8,128)(2,1)} %collective-permute-done.3, bf16[8,32,2048]{2,1,0:T(8,128)(2,1)S(1)} %get-tuple-element.8), kind=kLoop, calls=%fused_computation | loop fusion | flops 1048576 | bytes 1572864 | tf_op jit(solution)/shard_map/convert_element_type | solution.py:238
  38.9 1.6 %collective-permute-start.4 = (bf16[2,32,2048]{2,1,0:T(8,128)(2,1)S(1)}, bf16[2,32,2048]{2,1,0:T(8,128)(2,1)S(1)}, u32[]{:S(2)}, u32[]{:S(2)}) collective-permute-start(bf16[2,32,2048]{2,1,0:T(8,128)(2,1)S(1)} %slice.77), channel_id=1, source_target_pairs={{0,16},{4,20},{8,24},{12,28},{16,0},{20,4},{24,8},{28,12},{1,17},{... | collective-permute-start | bytes 786440 | tf_op jit(solution)/shard_map/ppermute | solution.py:218
  40.6 1.6 %copy-done.6 = bf16[8,64,2048]{2,1,0:T(8,128)(2,1)S(1)} copy-done((bf16[8,64,2048]{2,1,0:T(8,128)(2,1)S(1)}, bf16[8,64,2048]{2,1,0:T(8,128)(2,1)}, u32[]{:S(2)}) %copy-start.6) | copy-done | bytes 2097176
  42.2 13.5 %weights.1 = f32[144,96]{1,0:T(8,128)S(1)} custom-call(s32[32]{0:T(128)S(1)} %bitcast.17, s32[32]{0:T(128)S(1)} %and_select_fusion.chunks_ref, s32[2]{0:T(128)S(1)} %copy-done.5, s32[32,8,128]{2,1,0:T(8,128)S(1)} %copy-done.1, f32[8,4096]{1,0:T(8,128)S(1)} %pad.4.points_ref, bf16[64,4096]{1,0:T(8,128)(2,1)S(1)} %copy-done.8, ...), custom_call_target="tpu_custom_call" | custom-call | flops 5368709120 | bytes 10000000 | tf_op jit(solution)/shard_map/weights/pallas_call | solution.py:323
  55.6 0.2 collective-permute-start.6
  55.8 0.1 add_convert_fusion.3
  55.9 1.5 %collective-permute-start.2 = (bf16[1,32,2048]{2,1,0:T(8,128)(2,1)S(1)}, bf16[1,32,2048]{2,1,0:T(8,128)(2,1)S(1)}, u32[]{:S(2)}, u32[]{:S(2)}) collective-permute-start(bf16[1,32,2048]{2,1,0:T(8,128)(2,1)S(1)} %slice.75), channel_id=1, source_target_pairs={{0,16},{4,20},{8,24},{12,28},{16,0},{20,4},{24,8},{28,12},{1,17},{... | collective-permute-start | bytes 393224 | tf_op jit(solution)/shard_map/ppermute | solution.py:218
  57.4 1.0 %collective-permute-start.7 = (f32[144,96]{1,0:T(8,128)S(1)}, f32[144,96]{1,0:T(8,128)S(1)}, u32[]{:S(2)}, u32[]{:S(2)}) collective-permute-start(f32[144,96]{1,0:T(8,128)S(1)} %add.50), channel_id=1, source_target_pairs={{0,8},{4,12},{8,0},{12,4},{16,24},{20,28},{24,16},{28,20},{1,9},{5... | collective-permute-start | bytes 165896 | tf_op jit(solution)/shard_map/ppermute | solution.py:218
  58.4 0.1 add_convert_fusion.2
  58.5 1.1 %collective-permute-start.5 = (bf16[1,32,2048]{2,1,0:T(8,128)(2,1)S(1)}, bf16[1,32,2048]{2,1,0:T(8,128)(2,1)S(1)}, u32[]{:S(2)}, u32[]{:S(2)}) collective-permute-start(bf16[1,32,2048]{2,1,0:T(8,128)(2,1)S(1)} %slice.79), channel_id=1, source_target_pairs={{0,8},{4,12},{8,0},{12,4},{16,24},{20,28},{24,16},{28,20},{1,9},{5... | collective-permute-start | bytes 393224 | tf_op jit(solution)/shard_map/ppermute | solution.py:218
  59.6 2.9 %collective-permute-done.7 = f32[144,96]{1,0:T(8,128)S(1)} collective-permute-done((f32[144,96]{1,0:T(8,128)S(1)}, f32[144,96]{1,0:T(8,128)S(1)}, u32[]{:S(2)}, u32[]{:S(2)}) %collective-permute-start.7) | collective-permute-done | bytes 55328 | tf_op jit(solution)/shard_map/ppermute | solution.py:218
  62.5 1.0 %collective-permute-start.8 = (f32[144,96]{1,0:T(8,128)S(1)}, f32[144,96]{1,0:T(8,128)S(1)}, u32[]{:S(2)}, u32[]{:S(2)}) collective-permute-start(f32[144,96]{1,0:T(8,128)S(1)} %add.51), channel_id=1, source_target_pairs={{0,16},{4,20},{8,24},{12,28},{16,0},{20,4},{24,8},{28,12},{1,17},{... | collective-permute-start | bytes 165896 | tf_op jit(solution)/shard_map/ppermute | solution.py:218
  63.5 3.4 %collective-permute-done.8 = f32[144,96]{1,0:T(8,128)S(1)} collective-permute-done((f32[144,96]{1,0:T(8,128)S(1)}, f32[144,96]{1,0:T(8,128)S(1)}, u32[]{:S(2)}, u32[]{:S(2)}) %collective-permute-start.8) | collective-permute-done | bytes 55328 | tf_op jit(solution)/shard_map/ppermute | solution.py:218
  66.9 1.5 %collective-permute-start.9 = (f32[144,96]{1,0:T(8,128)S(1)}, f32[144,96]{1,0:T(8,128)S(1)}, u32[]{:S(2)}, u32[]{:S(2)}) collective-permute-start(f32[144,96]{1,0:T(8,128)S(1)} %add.52), channel_id=1, source_target_pairs={{0,1},{1,0},{2,3},{3,2},{4,5},{5,4},{6,7},{7,6},{8,9},{9,8},{10,11... | collective-permute-start | bytes 165896 | tf_op jit(solution)/shard_map/ppermute | solution.py:218
  68.5 2.8 %collective-permute-done.9 = f32[144,96]{1,0:T(8,128)S(1)} collective-permute-done((f32[144,96]{1,0:T(8,128)S(1)}, f32[144,96]{1,0:T(8,128)S(1)}, u32[]{:S(2)}, u32[]{:S(2)}) %collective-permute-start.9) | collective-permute-done | bytes 55328 | tf_op jit(solution)/shard_map/ppermute | solution.py:218
  71.4 3.1 %collective-permute-start.10 = (f32[144,96]{1,0:T(8,128)S(1)}, f32[144,96]{1,0:T(8,128)S(1)}, u32[]{:S(2)}, u32[]{:S(2)}) collective-permute-start(f32[144,96]{1,0:T(8,128)S(1)} %add.53), channel_id=1, source_target_pairs={{0,2},{1,3},{2,0},{3,1},{4,6},{5,7},{6,4},{7,5},{8,10},{9,11},{10,... | collective-permute-start | bytes 165896 | tf_op jit(solution)/shard_map/ppermute | solution.py:218
  74.5 0.8 maximum_bitcast_fusion
  75.3 1.5 %collective-permute-done.10 = f32[144,96]{1,0:T(8,128)S(1)} collective-permute-done((f32[144,96]{1,0:T(8,128)S(1)}, f32[144,96]{1,0:T(8,128)S(1)}, u32[]{:S(2)}, u32[]{:S(2)}) %collective-permute-start.10) | collective-permute-done | bytes 55328 | tf_op jit(solution)/shard_map/ppermute | solution.py:218
  76.9 0.1 slice_add_fusion
  77.0 0.6 slice.84
  77.6 0.7 slice_reduce_fusion.1
  78.3 0.7 slice_reduce_fusion
  79.0 0.7 copy.22
  (38 shorter events, 0.2 us)
Async XLA Ops:
  7.2 33.4 %all-gather.2.cloned.1.call-start = ((), (), s32[]{:S(2)}) async-start(), calls=%async_computation | async-start | bytes 2359296 | tf_op jit(solution)/shard_map/all_gather | solution.py:255
  15.1 0.9 %copy-start = (s32[32,8,128]{2,1,0:T(8,128)S(1)}, s32[32,8,128]{2,1,0:T(8,128)}, u32[]{:S(2)}) copy-start(s32[32,8,128]{2,1,0:T(8,128)} %compact.1.meta_ref) | copy-start | bytes 393220
  16.0 0.7 copy-start.2
  16.7 0.7 copy-start.4
  17.4 1.0 %copy-start.7 = (bf16[64,4096]{1,0:T(8,128)(2,1)S(1)}, bf16[64,4096]{1,0:T(8,128)(2,1)}, u32[]{:S(2)}) copy-start(bf16[64,4096]{1,0:T(8,128)(2,1)} %cot_ref.3) | copy-start | bytes 1572868
  18.4 0.7 copy-start.9
  29.7 2.2 %copy-start.3 = (bf16[64,80]{1,0:T(8,128)(2,1)S(1)}, bf16[64,80]{1,0:T(8,128)(2,1)}, u32[]{:S(2)}) copy-start(bf16[64,80]{1,0:T(8,128)(2,1)} %wout_ref.1) | copy-start | bytes 30724
  30.5 2.4 %collective-permute-start = (bf16[4,32,2048]{2,1,0:T(8,128)(2,1)}, bf16[4,32,2048]{2,1,0:T(8,128)(2,1)}, u32[]{:S(2)}, u32[]{:S(2)}) collective-permute-start(bf16[4,32,2048]{2,1,0:T(8,128)(2,1)} %slice.55), channel_id=1, source_target_pairs={{0,4},{4,0},{8,12},{12,8},{16,20},{20,16},{24,28},{28,24},{1,5},{5... | collective-permute-start | bytes 1572872 | tf_op jit(solution)/shard_map/ppermute | solution.py:218
  31.8 5.9 %collective-permute-start.3 = (bf16[4,32,2048]{2,1,0:T(8,128)(2,1)}, bf16[4,32,2048]{2,1,0:T(8,128)(2,1)}, u32[]{:S(2)}, u32[]{:S(2)}) collective-permute-start(bf16[4,32,2048]{2,1,0:T(8,128)(2,1)} %slice.61), channel_id=1, source_target_pairs={{0,4},{4,0},{8,12},{12,8},{16,20},{20,16},{24,28},{28,24},{1,5},{5... | collective-permute-start | bytes 1572872 | tf_op jit(solution)/shard_map/ppermute | solution.py:218
  32.0 8.6 %copy-start.1 = (s32[32,8,128]{2,1,0:T(8,128)S(1)}, s32[32,8,128]{2,1,0:T(8,128)}, u32[]{:S(2)}) copy-start(s32[32,8,128]{2,1,0:T(8,128)} %compact.1.meta_ref) | copy-start | bytes 393220
  32.0 8.6 %copy-start.5 = (s32[2]{0:T(128)S(1)}, s32[2]{0:T(128)}, u32[]{:S(2)}) copy-start(s32[2]{0:T(128)} %pad_add_fusion.slab_ref) | copy-start | bytes 28
  32.0 8.6 %copy-start.8 = (bf16[64,4096]{1,0:T(8,128)(2,1)S(1)}, bf16[64,4096]{1,0:T(8,128)(2,1)}, u32[]{:S(2)}) copy-start(bf16[64,4096]{1,0:T(8,128)(2,1)} %cot_ref.3) | copy-start | bytes 1572868
  32.0 8.6 %copy-start.10 = (s32[1,32]{1,0:T(1,128)S(1)}, s32[1,32]{1,0:T(1,128)}, u32[]{:S(2)}) copy-start(s32[1,32]{1,0:T(1,128)} %param.14) | copy-start | bytes 388
  34.1 4.8 %copy-start.11 = (bf16[4,32,2048]{2,1,0:T(8,128)(2,1)}, bf16[4,32,2048]{2,1,0:T(8,128)(2,1)S(1)}, u32[]{:S(2)}) copy-start(bf16[4,32,2048]{2,1,0:T(8,128)(2,1)S(1)} %add_convert_fusion.1) | copy-start | bytes 1572868
  34.9 20.9 %collective-permute-start.1 = (bf16[2,32,2048]{2,1,0:T(8,128)(2,1)}, bf16[2,32,2048]{2,1,0:T(8,128)(2,1)S(1)}, u32[]{:S(2)}, u32[]{:S(2)}) collective-permute-start(bf16[2,32,2048]{2,1,0:T(8,128)(2,1)} %slice.73), channel_id=1, source_target_pairs={{0,8},{4,12},{8,0},{12,4},{16,24},{20,28},{24,16},{28,20},{1,9},{5... | collective-permute-start | bytes 786440 | tf_op jit(solution)/shard_map/ppermute | solution.py:218
  38.9 19.5 %collective-permute-start.4 = (bf16[2,32,2048]{2,1,0:T(8,128)(2,1)S(1)}, bf16[2,32,2048]{2,1,0:T(8,128)(2,1)S(1)}, u32[]{:S(2)}, u32[]{:S(2)}) collective-permute-start(bf16[2,32,2048]{2,1,0:T(8,128)(2,1)S(1)} %slice.77), channel_id=1, source_target_pairs={{0,16},{4,20},{8,24},{12,28},{16,0},{20,4},{24,8},{28,12},{1,17},{... | collective-permute-start | bytes 786440 | tf_op jit(solution)/shard_map/ppermute | solution.py:218
  40.6 1.6 %copy-start.6 = (bf16[8,64,2048]{2,1,0:T(8,128)(2,1)S(1)}, bf16[8,64,2048]{2,1,0:T(8,128)(2,1)}, u32[]{:S(2)}) copy-start(bf16[8,64,2048]{2,1,0:T(8,128)(2,1)} %all-gather.2.cloned.1.call-done.latent_ref) | copy-start | bytes 6291460
  42.1 13.6 %copy-start.12 = (bf16[4,32,2048]{2,1,0:T(8,128)(2,1)S(1)}, bf16[4,32,2048]{2,1,0:T(8,128)(2,1)}, u32[]{:S(2)}) copy-start(bf16[4,32,2048]{2,1,0:T(8,128)(2,1)} %copy-done.11) | copy-start | bytes 1572868
  55.6 1.7 %collective-permute-start.6 = (f32[144,96]{1,0:T(8,128)S(1)}, f32[144,96]{1,0:T(8,128)S(1)}, u32[]{:S(2)}, u32[]{:S(2)}) collective-permute-start(f32[144,96]{1,0:T(8,128)S(1)} %weights.1), channel_id=1, source_target_pairs={{0,4},{4,0},{8,12},{12,8},{16,20},{20,16},{24,28},{28,24},{1,5},{5... | collective-permute-start | bytes 165896 | tf_op jit(solution)/shard_map/ppermute | solution.py:218
  55.9 7.6 %collective-permute-start.2 = (bf16[1,32,2048]{2,1,0:T(8,128)(2,1)S(1)}, bf16[1,32,2048]{2,1,0:T(8,128)(2,1)S(1)}, u32[]{:S(2)}, u32[]{:S(2)}) collective-permute-start(bf16[1,32,2048]{2,1,0:T(8,128)(2,1)S(1)} %slice.75), channel_id=1, source_target_pairs={{0,16},{4,20},{8,24},{12,28},{16,0},{20,4},{24,8},{28,12},{1,17},{... | collective-permute-start | bytes 393224 | tf_op jit(solution)/shard_map/ppermute | solution.py:218
  57.4 5.1 %collective-permute-start.7 = (f32[144,96]{1,0:T(8,128)S(1)}, f32[144,96]{1,0:T(8,128)S(1)}, u32[]{:S(2)}, u32[]{:S(2)}) collective-permute-start(f32[144,96]{1,0:T(8,128)S(1)} %add.50), channel_id=1, source_target_pairs={{0,8},{4,12},{8,0},{12,4},{16,24},{20,28},{24,16},{28,20},{1,9},{5... | collective-permute-start | bytes 165896 | tf_op jit(solution)/shard_map/ppermute | solution.py:218
  58.5 10.0 %collective-permute-start.5 = (bf16[1,32,2048]{2,1,0:T(8,128)(2,1)S(1)}, bf16[1,32,2048]{2,1,0:T(8,128)(2,1)S(1)}, u32[]{:S(2)}, u32[]{:S(2)}) collective-permute-start(bf16[1,32,2048]{2,1,0:T(8,128)(2,1)S(1)} %slice.79), channel_id=1, source_target_pairs={{0,8},{4,12},{8,0},{12,4},{16,24},{20,28},{24,16},{28,20},{1,9},{5... | collective-permute-start | bytes 393224 | tf_op jit(solution)/shard_map/ppermute | solution.py:218
  62.5 4.4 %collective-permute-start.8 = (f32[144,96]{1,0:T(8,128)S(1)}, f32[144,96]{1,0:T(8,128)S(1)}, u32[]{:S(2)}, u32[]{:S(2)}) collective-permute-start(f32[144,96]{1,0:T(8,128)S(1)} %add.51), channel_id=1, source_target_pairs={{0,16},{4,20},{8,24},{12,28},{16,0},{20,4},{24,8},{28,12},{1,17},{... | collective-permute-start | bytes 165896 | tf_op jit(solution)/shard_map/ppermute | solution.py:218
  66.9 4.4 %collective-permute-start.9 = (f32[144,96]{1,0:T(8,128)S(1)}, f32[144,96]{1,0:T(8,128)S(1)}, u32[]{:S(2)}, u32[]{:S(2)}) collective-permute-start(f32[144,96]{1,0:T(8,128)S(1)} %add.52), channel_id=1, source_target_pairs={{0,1},{1,0},{2,3},{3,2},{4,5},{5,4},{6,7},{7,6},{8,9},{9,8},{10,11... | collective-permute-start | bytes 165896 | tf_op jit(solution)/shard_map/ppermute | solution.py:218
  71.4 5.5 %collective-permute-start.10 = (f32[144,96]{1,0:T(8,128)S(1)}, f32[144,96]{1,0:T(8,128)S(1)}, u32[]{:S(2)}, u32[]{:S(2)}) collective-permute-start(f32[144,96]{1,0:T(8,128)S(1)} %add.53), channel_id=1, source_target_pairs={{0,2},{1,3},{2,0},{3,1},{4,6},{5,7},{6,4},{7,5},{8,10},{9,11},{10,... | collective-permute-start | bytes 165896 | tf_op jit(solution)/shard_map/ppermute | solution.py:218
Sparse Core Ops, SparseCore 0:
  9.9 30.4 all-gather.1
